TPU v7x, 32 devices: a whole 2x2x4 slice. The times are simulated.
32 devices in a mesh: blk: 8 (over y, x, core), feat: 4 (over z).
Axes of the slice: x: 2, y: 2, z: 4, core: 2. Of those that a mesh axis runs over, the one named last changes fastest.
Arguments:
- node_feats: bfloat16 [8192, 512], P('blk', 'feat'), may hold values from -6 to 6
- weight: bfloat16 [512, 512], P(None, 'feat'), may hold values from -0.25 to 0.25
- tile_value: bfloat16 [8, 5, 8, 128, 128], P('blk'), may hold values from -0.75 to 0.75
- tile_row: int32 [8, 5, 8], P('blk'), may hold values from 0 to 7
- tile_col: int32 [8, 5, 8], P('blk'), may hold values from 0 to 7
- tile_count: int32 [8, 5], P('blk'), may hold values from 2 to 8, as said below
- grad_out: bfloat16 [8192, 512], P('blk', 'feat'), may hold values from -6 to 6
Outputs:
- output_y: bfloat16 [8192, 512], P('blk', 'feat')
- grad_x: bfloat16 [8192, 512], P('blk', 'feat')
- grad_w: float32 [512, 512], P(None, 'feat')
Inputs may be any that keep to these rules, and one draw needn't show every extreme that they name: `tile_count`: in every draw one owner has all 8 slots live for every distance; owners differ in how many tiles they hold.
All inputs are finite; a program needn't handle non-finite values.
Results may differ from a plain program's by a relative error of at most 0.0062.
Values may be sent and summed in bfloat16 or wider, within the bound.
A program may use at most 64 MiB of HBM per device.

v0:
```python
import jax
import jax.numpy as jnp
from jax import lax
from jax.sharding import PartitionSpec as P


def shifted(block, axis, distance):
    devices = range(lax.axis_size(axis))
    route = [((i - distance) % len(devices), i) for i in devices]
    return lax.ppermute(block, axis, route)


def on_device(node_feats, weight, tile_value, tile_row, tile_col, tile_count, grad_out):
    tile_side = tile_value.shape[-1]
    blocks = node_feats.shape[0] // tile_side
    feat_width = weight.shape[1]
    offsets = tile_value.shape[1]
    reach_count = (offsets - 1) // 2
    slot_ids = jnp.arange(tile_value.shape[2], dtype=jnp.int32)
    block_ids = jnp.arange(blocks, dtype=jnp.int32)
    live_slots = slot_ids[None, :] < tile_count[0][:, None]
    row_onehot = (
        (tile_row[0][:, None, :] == block_ids[None, :, None]) & live_slots[:, None, :]
    ).astype(jnp.float32)
    col_onehot = (
        (tile_col[0][:, None, :] == block_ids[None, :, None]) & live_slots[:, None, :]
    ).astype(jnp.float32)
    full_feats = lax.all_gather(node_feats, "feat", axis=1, tiled=True)
    hidden = jnp.dot(full_feats, weight, preferred_element_type=jnp.float32).astype(jnp.bfloat16)
    panel_own = hidden.reshape(blocks, tile_side, feat_width)
    wanted_lists = {}
    picked = jnp.take(panel_own, tile_col[0, reach_count], axis=0)
    gather_product = jnp.einsum(
        "sij,sjf->sif", tile_value[0, reach_count], picked, preferred_element_type=jnp.float32
    )
    aggregate = jnp.einsum(
        "rs,sif->rif", row_onehot[reach_count], gather_product, precision=lax.Precision.HIGHEST
    )
    for distance in range(-reach_count, reach_count + 1):
        if distance != 0:
            offset = distance + reach_count
            wanted = shifted(tile_col[0, offset], "blk", distance)
            wanted_lists[distance] = wanted
            sent_blocks = jnp.take(panel_own, wanted, axis=0)
            arrived = shifted(sent_blocks, "blk", -distance)
            product = jnp.einsum(
                "sij,sjf->sif", tile_value[0, offset], arrived, preferred_element_type=jnp.float32
            )
            aggregate = aggregate + jnp.einsum(
                "rs,sif->rif", row_onehot[offset], product, precision=lax.Precision.HIGHEST
            )
    preact = aggregate.reshape(blocks * tile_side, feat_width) + hidden.astype(jnp.float32)
    output_y = jax.nn.silu(preact).astype(jnp.bfloat16)
    sigmoid_pre = jax.nn.sigmoid(preact)
    slope_term = sigmoid_pre * (1.0 + preact * (1.0 - sigmoid_pre))
    grad_pre = (grad_out.astype(jnp.float32) * slope_term).astype(jnp.bfloat16)
    grad_blocks = grad_pre.reshape(blocks, tile_side, feat_width)

    def slot_products(offset):
        picked = jnp.take(grad_blocks, tile_row[0, offset], axis=0)
        return jnp.einsum(
            "sji,sjf->sif", tile_value[0, offset], picked, preferred_element_type=jnp.float32
        )

    transposed = jnp.einsum(
        "cs,sif->cif",
        col_onehot[reach_count],
        slot_products(reach_count),
        precision=lax.Precision.HIGHEST,
    )
    for distance in range(-reach_count, reach_count + 1):
        if distance != 0:
            offset = distance + reach_count
            masked = slot_products(offset) * live_slots[offset][:, None, None].astype(jnp.float32)
            received = shifted(masked, "blk", distance)
            target_onehot = (wanted_lists[distance][None, :] == block_ids[:, None]).astype(
                jnp.float32
            )
            transposed = transposed + jnp.einsum(
                "cs,sif->cif", target_onehot, received, precision=lax.Precision.HIGHEST
            )
    grad_hidden = (
        grad_pre.astype(jnp.float32) + transposed.reshape(blocks * tile_side, feat_width)
    ).astype(jnp.bfloat16)
    weight_term = lax.dot_general(
        full_feats, grad_hidden, (((0,), (0,)), ((), ())), preferred_element_type=jnp.float32
    )
    grad_w = lax.psum(weight_term, "blk")
    partial_grad = lax.dot_general(
        grad_hidden, weight, (((1,), (1,)), ((), ())), preferred_element_type=jnp.float32
    )
    grad_x = lax.psum_scatter(partial_grad, "feat", scatter_dimension=1, tiled=True).astype(
        jnp.bfloat16
    )
    return (output_y, grad_x, grad_w)


def solution(mesh):
    return jax.shard_map(
        on_device,
        mesh=mesh,
        in_specs=(
            P("blk", "feat"),
            P(None, "feat"),
            P("blk", None, None, None, None),
            P("blk", None, None),
            P("blk", None, None),
            P("blk", None),
            P("blk", "feat"),
        ),
        out_specs=(P("blk", "feat"), P("blk", "feat"), P(None, "feat")),
        check_vma=False,
    )
```

profile of v0, /device:TPU:0, one launch (start us, length us, event | category | flops | bytes accessed | tf_op | source)
XLA Modules:
  0.0 216.4 jit_solution(13034620834880448403)
XLA Ops:
  8.7 3.9 %collective-permute-start = (s32[8]{0:T(128)S(1)}, s32[8]{0:T(128)S(1)}, u32[]{:S(2)}, u32[]{:S(2)}) collective-permute-start(s32[8]{0:T(128)S(1)} %get-tuple-element.32), channel_id=1, source_target_pairs={{8,0},{12,4},{16,8},{20,12},{24,16},{28,20},{0,24},{4,28},{9,1},{1... | collective-permute-start | bytes 104 | tf_op jit(solution)/shard_map/ppermute | solution.py:10
  15.1 1.3 compare_and_fusion.2
  22.6 19.6 %all-gather.2.cloned.1.call-done = bf16[1024,512]{1,0:T(8,128)(2,1)} async-done(((bf16[1024,128]{1,0:T(8,128)(2,1)}), bf16[1024,512]{1,0:T(8,128)(2,1)}) %all-gather.2.cloned.1.call-update) | async-done | bytes 1048592 | tf_op jit(solution)/shard_map/all_gather | solution.py:28
  42.2 1.7 convolution_convert_fusion
  49.6 2.6 %collective-permute-start.5 = (bf16[8,128,128]{2,1,0:T(8,128)(2,1)}, bf16[8,128,128]{2,1,0:T(8,128)(2,1)}, u32[]{:S(2)}, u32[]{:S(2)}) collective-permute-start(bf16[8,128,128]{2,1,0:T(8,128)(2,1)} %broadcast_select_fusion.1), channel_id=1, source_target_pairs={{4,0},{8,4},{12,8},{16,12},{20,16},{24,20},{28,24},{0,28},{5,1},{9... | collective-permute-start | bytes 786440 | tf_op jit(solution)/shard_map/ppermute | solution.py:10
  53.7 1.3 collective-permute-start.7
  55.4 1.3 fusion.25
  56.7 1.3 fusion.21
  58.0 1.0 copy.14
  59.0 1.0 copy.15
  60.0 1.3 fusion.17
  61.3 1.0 copy.16
  62.3 1.8 collective-permute-done.7
  64.4 1.0 copy.17
  68.5 1.0 multiply_convert_fusion
  71.0 0.9 multiply_bitcast_fusion.3
  71.9 1.5 collective-permute-start.8
  75.3 0.9 multiply_bitcast_fusion.1
  81.3 2.4 %collective-permute-start.9 = (f32[8,128,128]{2,0,1:T(8,128)S(1)}, f32[8,128,128]{2,0,1:T(8,128)S(1)}, u32[]{:S(2)}, u32[]{:S(2)}) collective-permute-start(f32[8,128,128]{2,0,1:T(8,128)S(1)} %multiply_bitcast_fusion.2), channel_id=1, source_target_pairs={{4,0},{8,4},{12,8},{16,12},{20,16},{24,20},{28,24},{0,28},{5,1},{9... | collective-permute-start | bytes 1572872 | tf_op jit(solution)/shard_map/ppermute | solution.py:10
  84.1 9.4 %collective-permute-done.10 = f32[8,128,128]{2,0,1:T(8,128)} collective-permute-done((f32[8,128,128]{2,0,1:T(8,128)}, f32[8,128,128]{2,0,1:T(8,128)}, u32[]{:S(2)}, u32[]{:S(2)}) %collective-permute-start.10) | collective-permute-done | bytes 524320 | tf_op jit(solution)/shard_map/ppermute | solution.py:10
  93.4 1.4 fusion.65
  94.8 3.1 %collective-permute-done.11 = f32[8,128,128]{2,0,1:T(8,128)} collective-permute-done((f32[8,128,128]{2,0,1:T(8,128)}, f32[8,128,128]{2,0,1:T(8,128)}, u32[]{:S(2)}, u32[]{:S(2)}) %collective-permute-start.11) | collective-permute-done | bytes 524320 | tf_op jit(solution)/shard_map/ppermute | solution.py:10
  97.9 1.4 fusion.68
  99.4 1.4 convolution_add_fusion.1
  100.8 5.3 %collective-permute-done.9 = f32[8,128,128]{2,0,1:T(8,128)S(1)} collective-permute-done((f32[8,128,128]{2,0,1:T(8,128)S(1)}, f32[8,128,128]{2,0,1:T(8,128)S(1)}, u32[]{:S(2)}, u32[]{:S(2)}) %collective-permute-start.9) | collective-permute-done | bytes 524320 | tf_op jit(solution)/shard_map/ppermute | solution.py:10
  106.7 1.0 copy-done.2
  107.7 1.0 convolution_bitcast_fusion
  108.8 1.8 fusion.89
  110.6 52.1 %all-reduce.2.cloned.1.call-done = f32[512,128]{0,1:T(8,128)} async-done(((f32[512,128]{0,1:T(8,128)}), f32[512,128]{0,1:T(8,128)}) %all-reduce.2.cloned.1.call-update) | async-done | bytes 262160 | tf_op jit(solution)/shard_map/psum | solution.py:88
  162.7 1.8 copy.12
  164.5 43.6 %reduce-scatter.2.cloned.1.call-done = f32[1024,128]{1,0:T(8,128)} async-done(((f32[1024,512]{1,0:T(8,128)}), f32[1024,128]{1,0:T(8,128)}) %reduce-scatter.2.cloned.1.call-update) | async-done | bytes 524304 | tf_op jit(solution)/shard_map/reduce_scatter | solution.py:92
  208.1 1.8 convert_element_type.89
  (141 shorter events, 30.1 us)
Async XLA Ops:
  7.2 35.1 %copy-start = (bf16[512,128]{1,0:T(8,128)(2,1)S(1)}, bf16[512,128]{1,0:T(8,128)(2,1)}, u32[]{:S(2)}) copy-start(bf16[512,128]{1,0:T(8,128)(2,1)} %param.10) | copy-start | bytes 393220
  7.2 35.1 %all-gather.2.cloned.1.call-start = ((), (), s32[]{:S(2)}) async-start(), calls=%async_computation.1 | async-start | bytes 1310720 | tf_op jit(solution)/shard_map/all_gather | solution.py:28
  7.9 154.8 %all-reduce.2.cloned.1.call-start = ((), (), s32[]{:S(2)}) async-start(), calls=%async_computation.3 | async-start | bytes 524288 | tf_op jit(solution)/shard_map/psum | solution.py:88
  8.7 11.6 %collective-permute-start = (s32[8]{0:T(128)S(1)}, s32[8]{0:T(128)S(1)}, u32[]{:S(2)}, u32[]{:S(2)}) collective-permute-start(s32[8]{0:T(128)S(1)} %get-tuple-element.32), channel_id=1, source_target_pairs={{8,0},{12,4},{16,8},{20,12},{24,16},{28,20},{0,24},{4,28},{9,1},{1... | collective-permute-start | bytes 104 | tf_op jit(solution)/shard_map/ppermute | solution.py:10
  12.6 7.7 %collective-permute-start.2 = (s32[8]{0:T(128)S(1)}, s32[8]{0:T(128)S(1)}, u32[]{:S(2)}, u32[]{:S(2)}) collective-permute-start(s32[8]{0:T(128)S(1)} %get-tuple-element.31), channel_id=1, source_target_pairs={{4,0},{8,4},{12,8},{16,12},{20,16},{24,20},{28,24},{0,28},{5,1},{9... | collective-permute-start | bytes 104 | tf_op jit(solution)/shard_map/ppermute | solution.py:10
  12.6 7.7 %collective-permute-start.4 = (s32[8]{0:T(128)S(1)}, s32[8]{0:T(128)S(1)}, u32[]{:S(2)}, u32[]{:S(2)}) collective-permute-start(s32[8]{0:T(128)S(1)} %get-tuple-element.30), channel_id=1, source_target_pairs={{28,0},{0,4},{4,8},{8,12},{12,16},{16,20},{20,24},{24,28},{29,1},{... | collective-permute-start | bytes 104 | tf_op jit(solution)/shard_map/ppermute | solution.py:10
  13.1 7.8 %collective-permute-start.6 = (s32[8]{0:T(128)S(1)}, s32[8]{0:T(128)S(1)}, u32[]{:S(2)}, u32[]{:S(2)}) collective-permute-start(s32[8]{0:T(128)S(1)} %get-tuple-element.29), channel_id=1, source_target_pairs={{24,0},{28,4},{0,8},{4,12},{8,16},{12,20},{16,24},{20,28},{25,1},{... | collective-permute-start | bytes 104 | tf_op jit(solution)/shard_map/ppermute | solution.py:10
  20.2 25.7 %copy-start.19 = (s32[8]{0:T(128)}, s32[8]{0:T(128)S(1)}, u32[]{:S(2)}) copy-start(s32[8]{0:T(128)S(1)} %collective-permute-done) | copy-start | bytes 100
  20.3 25.7 %copy-start.27 = (s32[8]{0:T(128)}, s32[8]{0:T(128)S(1)}, u32[]{:S(2)}) copy-start(s32[8]{0:T(128)S(1)} %collective-permute-done.2) | copy-start | bytes 100
  20.3 25.7 %copy-start.23 = (s32[8]{0:T(128)}, s32[8]{0:T(128)S(1)}, u32[]{:S(2)}) copy-start(s32[8]{0:T(128)S(1)} %collective-permute-done.4) | copy-start | bytes 100
  20.9 25.0 %copy-start.21 = (s32[8]{0:T(128)}, s32[8]{0:T(128)S(1)}, u32[]{:S(2)}) copy-start(s32[8]{0:T(128)S(1)} %collective-permute-done.6) | copy-start | bytes 100
  22.6 23.4 %copy-start.1 = (bf16[1,5,8,128,128]{4,3,2,1,0:T(8,128)(2,1)S(1)}, bf16[1,5,8,128,128]{4,3,2,1,0:T(8,128)(2,1)}, u32[]{:S(2)}) copy-start(bf16[1,5,8,128,128]{4,3,2,1,0:T(8,128)(2,1)} %param.11) | copy-start | bytes 3932164
  44.6 10.8 %collective-permute-start.1 = (bf16[8,128,128]{2,1,0:T(8,128)(2,1)S(1)}, bf16[8,128,128]{2,1,0:T(8,128)(2,1)}, u32[]{:S(2)}, u32[]{:S(2)}) collective-permute-start(bf16[8,128,128]{2,1,0:T(8,128)(2,1)S(1)} %broadcast_select_fusion.3), channel_id=1, source_target_pairs={{24,0},{28,4},{0,8},{4,12},{8,16},{12,20},{16,24},{20,28},{25,1},{... | collective-permute-start | bytes 786440 | tf_op jit(solution)/shard_map/ppermute | solution.py:10
  46.7 6.2 %copy-start.25 = (pred[8]{0:T(512)(128)(4,1)S(1)}, pred[8]{0:T(512)(128)(4,1)}, u32[]{:S(2)}) copy-start(pred[8]{0:T(512)(128)(4,1)} %compare_and_fusion.5) | copy-start | bytes 28
  48.0 8.6 %collective-permute-start.3 = (bf16[8,128,128]{2,1,0:T(8,128)(2,1)S(1)}, bf16[8,128,128]{2,1,0:T(8,128)(2,1)}, u32[]{:S(2)}, u32[]{:S(2)}) collective-permute-start(bf16[8,128,128]{2,1,0:T(8,128)(2,1)S(1)} %broadcast_select_fusion.2), channel_id=1, source_target_pairs={{28,0},{0,4},{4,8},{8,12},{12,16},{16,20},{20,24},{24,28},{29,1},{... | collective-permute-start | bytes 786440 | tf_op jit(solution)/shard_map/ppermute | solution.py:10
  49.6 10.4 %collective-permute-start.5 = (bf16[8,128,128]{2,1,0:T(8,128)(2,1)}, bf16[8,128,128]{2,1,0:T(8,128)(2,1)}, u32[]{:S(2)}, u32[]{:S(2)}) collective-permute-start(bf16[8,128,128]{2,1,0:T(8,128)(2,1)} %broadcast_select_fusion.1), channel_id=1, source_target_pairs={{4,0},{8,4},{12,8},{16,12},{20,16},{24,20},{28,24},{0,28},{5,1},{9... | collective-permute-start | bytes 786440 | tf_op jit(solution)/shard_map/ppermute | solution.py:10
  53.7 10.4 %collective-permute-start.7 = (bf16[8,128,128]{2,1,0:T(8,128)(2,1)}, bf16[8,128,128]{2,1,0:T(8,128)(2,1)S(1)}, u32[]{:S(2)}, u32[]{:S(2)}) collective-permute-start(bf16[8,128,128]{2,1,0:T(8,128)(2,1)} %broadcast_select_fusion), channel_id=1, source_target_pairs={{8,0},{12,4},{16,8},{20,12},{24,16},{28,20},{0,24},{4,28},{9,1},{1... | collective-permute-start | bytes 786440 | tf_op jit(solution)/shard_map/ppermute | solution.py:10
  62.3 3.1 %copy-start.3 = (f32[8,128,128]{1,0,2:T(8,128)S(1)}, f32[8,128,128]{1,0,2:T(8,128)}, u32[]{:S(2)}) copy-start(f32[8,128,128]{1,0,2:T(8,128)} %copy.14) | copy-start | bytes 1572868
  70.9 3.7 %copy-start.16 = (pred[8]{0:T(512)(128)(4,1)S(1)}, pred[8]{0:T(512)(128)(4,1)}, u32[]{:S(2)}) copy-start(pred[8]{0:T(512)(128)(4,1)} %get-tuple-element.27) | copy-start | bytes 28
  71.9 27.5 %collective-permute-start.8 = (f32[8,128,128]{2,0,1:T(8,128)}, f32[8,128,128]{2,0,1:T(8,128)}, u32[]{:S(2)}, u32[]{:S(2)}) collective-permute-start(f32[8,128,128]{2,0,1:T(8,128)} %multiply_bitcast_fusion.3), channel_id=1, source_target_pairs={{8,0},{12,4},{16,8},{20,12},{24,16},{28,20},{0,24},{4,28},{9,1},{1... | collective-permute-start | bytes 1572872 | tf_op jit(solution)/shard_map/ppermute | solution.py:10
  76.2 17.2 %collective-permute-start.10 = (f32[8,128,128]{2,0,1:T(8,128)}, f32[8,128,128]{2,0,1:T(8,128)}, u32[]{:S(2)}, u32[]{:S(2)}) collective-permute-start(f32[8,128,128]{2,0,1:T(8,128)} %multiply_bitcast_fusion.1), channel_id=1, source_target_pairs={{28,0},{0,4},{4,8},{8,12},{12,16},{16,20},{20,24},{24,28},{29,1},{... | collective-permute-start | bytes 1572872 | tf_op jit(solution)/shard_map/ppermute | solution.py:10
  77.4 2.5 %copy-start.14 = (pred[8]{0:T(512)(128)(4,1)S(1)}, pred[8]{0:T(512)(128)(4,1)}, u32[]{:S(2)}) copy-start(pred[8]{0:T(512)(128)(4,1)} %get-tuple-element.23) | copy-start | bytes 28
  77.7 2.6 %copy-start.13 = (pred[8]{0:T(512)(128)(4,1)S(1)}, pred[8]{0:T(512)(128)(4,1)}, u32[]{:S(2)}) copy-start(pred[8]{0:T(512)(128)(4,1)} %get-tuple-element.7) | copy-start | bytes 28
  78.6 19.4 %collective-permute-start.11 = (f32[8,128,128]{2,0,1:T(8,128)}, f32[8,128,128]{2,0,1:T(8,128)}, u32[]{:S(2)}, u32[]{:S(2)}) collective-permute-start(f32[8,128,128]{2,0,1:T(8,128)} %multiply_bitcast_fusion), channel_id=1, source_target_pairs={{24,0},{28,4},{0,8},{4,12},{8,16},{12,20},{16,24},{20,28},{25,1},{... | collective-permute-start | bytes 1572872 | tf_op jit(solution)/shard_map/ppermute | solution.py:10
  80.8 2.8 %copy-start.8 = (pred[1,8]{1,0:T(4,128)(4,1)S(1)}, pred[1,8]{1,0:T(4,128)(4,1)}, u32[]{:S(2)}) copy-start(pred[1,8]{1,0:T(4,128)(4,1)} %get-tuple-element.34) | copy-start | bytes 28
  80.8 2.8 %copy-start.18 = (s32[1,8]{1,0:T(1,128)S(1)}, s32[1,8]{1,0:T(1,128)}, u32[]{:S(2)}) copy-start(s32[1,8]{1,0:T(1,128)} %slice.130) | copy-start | bytes 100
  81.0 12.4 %copy-start.24 = (s32[8]{0:T(128)S(1)}, s32[8]{0:T(128)}, u32[]{:S(2)}) copy-start(s32[8]{0:T(128)} %copy-done.23) | copy-start | bytes 100
  81.3 16.7 %copy-start.22 = (s32[8]{0:T(128)S(1)}, s32[8]{0:T(128)}, u32[]{:S(2)}) copy-start(s32[8]{0:T(128)} %copy-done.21) | copy-start | bytes 100
  81.3 24.8 %collective-permute-start.9 = (f32[8,128,128]{2,0,1:T(8,128)S(1)}, f32[8,128,128]{2,0,1:T(8,128)S(1)}, u32[]{:S(2)}, u32[]{:S(2)}) collective-permute-start(f32[8,128,128]{2,0,1:T(8,128)S(1)} %multiply_bitcast_fusion.2), channel_id=1, source_target_pairs={{4,0},{8,4},{12,8},{16,12},{20,16},{24,20},{28,24},{0,28},{5,1},{9... | collective-permute-start | bytes 1572872 | tf_op jit(solution)/shard_map/ppermute | solution.py:10
  84.1 15.3 %copy-start.20 = (s32[8]{0:T(128)S(1)}, s32[8]{0:T(128)}, u32[]{:S(2)}) copy-start(s32[8]{0:T(128)} %copy-done.19) | copy-start | bytes 100
  94.8 11.2 %copy-start.28 = (s32[8]{0:T(128)S(1)}, s32[8]{0:T(128)}, u32[]{:S(2)}) copy-start(s32[8]{0:T(128)} %copy-done.27) | copy-start | bytes 100
  108.8 99.3 %reduce-scatter.2.cloned.1.call-start = ((), (), s32[]{:S(2)}) async-start(), calls=%async_computation.2 | async-start | bytes 2621440 | tf_op jit(solution)/shard_map/reduce_scatter | solution.py:92
  (12 other events, 16.7 us)
Sparse Core Ops, SparseCore 0:
  9.5 32.6 all-gather.1
  108.9 53.7 all-reduce.1
  165.0 43.0 reduce-scatter.1
where the time goes:
time: 217 us; the launch traced here: 216 us
  waiting for transfers between devices  136 us (63%)
  local copies, waits for them, and re-layouts  19.5 us (9%)
  matrix products  17.6 us (8%)
  other arithmetic  14.8 us (7%)
  starting transfers between devices  14.4 us (7%)
  between operations  14.4 us (7%)
    psum x1, waiting for transfers between devices, on_device(): grad_w = lax.psum(weight_term, 'blk')  52.1 us
    reduce_scatter x1, waiting for transfers between devices, on_device(): lax.psum_scatter(partial_grad, 'feat', scatter_dimension=1, tiled=True)  43.6 us
    all_gather x1, waiting for transfers between devices, on_device(): full_feats = lax.all_gather(node_feats, 'feat', axis=1, tiled=True)  19.6 us
    ppermute x12, waiting for transfers between devices, shifted(): return lax.ppermute(block, axis, route)  19.6 us
    ppermute x12, starting transfers between devices, shifted(): return lax.ppermute(block, axis, route)  14.3 us
    unnamed x61, local copies, waits for them, and re-layouts  5.8 us
    dot_general x4, matrix products, on_device(): jnp.einsum('cs,sif->cif', target_onehot, received, precision=lax.Precisio...  4.6 us
  transfers between devices with their start and end apart: 15, of which 7 were waited for; matrix products, arithmetic and copies ran while one was open for 17% of the time, Pallas kernels for 0%

commit v1 on v0

--- a/solution.py
+++ b/solution.py
@@ -25,7 +25,9 @@
     col_onehot = (
         (tile_col[0][:, None, :] == block_ids[None, :, None]) & live_slots[:, None, :]
     ).astype(jnp.float32)
-    full_feats = lax.all_gather(node_feats, "feat", axis=1, tiled=True)
+    full_feats = jnp.concatenate(
+        lax.all_to_all(jnp.stack([node_feats] * lax.axis_size("feat")), "feat", 0, 0), axis=1
+    )
     hidden = jnp.dot(full_feats, weight, preferred_element_type=jnp.float32).astype(jnp.bfloat16)
     panel_own = hidden.reshape(blocks, tile_side, feat_width)
     wanted_lists = {}

time: 217 us -> 182 us (0.84)
  waiting for transfers between devices: 136 us -> 74.6 us
  local copies, waits for them, and re-layouts: 19.5 us -> 26.6 us
  matrix products: 17.6 us -> 24.5 us
  starting transfers between devices: 14.4 us -> 19.9 us
  other arithmetic: 14.8 us -> 19.1 us
    reduce_scatter x1, waiting for transfers between devices: 43.6 us -> 0.01 us  [on_device(): lax.psum_scatter(partial_grad, 'feat', scatter_dimension=1, tiled=True)]
    all_gather x1 -> x0, waiting for transfers between devices: 19.6 us -> none  [on_device(): full_feats = lax.all_gather(node_feats, 'feat', axis=1, tiled=True)]
    all_to_all x0 -> x1, waiting for transfers between devices: none -> 16.3 us  [on_device(): lax.all_to_all(jnp.stack([node_feats] * lax.axis_size('feat')), 'feat', 0...]
    ppermute x12, waiting for transfers between devices: 19.6 us -> 6.53 us  [shifted(): return lax.ppermute(block, axis, route)]
    all_to_all x0 -> x1, starting transfers between devices: none -> 6.48 us  [on_device(): lax.all_to_all(jnp.stack([node_feats] * lax.axis_size('feat')), 'feat', 0...]
    dot_general x5, matrix products: 1.74 us -> 5.4 us  [slot_products(): jnp.einsum('sji,sjf->sif', tile_value[0, offset], picked, preferred_eleme...]
    dot_general x5, local copies, waits for them, and re-layouts: 1.16 us -> 4.51 us  [slot_products(): jnp.einsum('sji,sjf->sif', tile_value[0, offset], picked, preferred_eleme...]
    mul x4, other arithmetic: 2.8 us -> 5.93 us  [on_device(): slot_products(offset)]
  transfers between devices with their start and end apart: 15 -> 15, of which waited for: 7 -> 4; matrix products, arithmetic and copies ran while one was open for 17% -> 28% of each run, Pallas kernels for 0% -> 0%
where the time goes in v1:
time: 182 us; the launch traced here: 181 us
  waiting for transfers between devices  74.6 us (41%)
  local copies, waits for them, and re-layouts  26.6 us (15%)
  matrix products  24.5 us (13%)
  starting transfers between devices  19.9 us (11%)
  other arithmetic  19.1 us (10%)
  between operations  16 us (9%)
    psum x1, waiting for transfers between devices, on_device(): grad_w = lax.psum(weight_term, 'blk')  51.8 us
    all_to_all x1, waiting for transfers between devices, on_device(): lax.all_to_all(jnp.stack([node_feats] * lax.axis_size('feat')), 'feat', 0...  16.3 us
    ppermute x12, starting transfers between devices, shifted(): return lax.ppermute(block, axis, route)  13.4 us
    ppermute x12, waiting for transfers between devices, shifted(): return lax.ppermute(block, axis, route)  6.53 us
    all_to_all x1, starting transfers between devices, on_device(): lax.all_to_all(jnp.stack([node_feats] * lax.axis_size('feat')), 'feat', 0...  6.48 us
    dot_general x4, local copies, waits for them, and re-layouts, on_device(): jnp.einsum('sij,sjf->sif', tile_value[0, offset], arrived, preferred_elem...  6.13 us
    mul x4, other arithmetic, on_device(): slot_products(offset)  5.93 us
    gather x5, local copies, waits for them, and re-layouts, slot_products(): picked = jnp.take(grad_blocks, tile_row[0, offset], axis=0)  5.78 us
  transfers between devices with their start and end apart: 15, of which 4 were waited for; matrix products, arithmetic and copies ran while one was open for 28% of the time, Pallas kernels for 0%

profile of v1, /device:TPU:0, one launch (start us, length us, event | category | flops | bytes accessed | tf_op | source)
XLA Modules:
  0.0 180.8 jit_solution(8185122592657683556)
XLA Ops:
  10.3 6.5 %all-to-all-start = ((bf16[4,1024,128]{1,2,0:T(8,128)(2,1)}), bf16[4,1024,128]{1,2,0:T(8,128)(2,1)S(1)}, u32[]{:S(2)}, u32[]{:S(2)}) async-start(bf16[4,1024,128]{1,2,0:T(8,128)(2,1)} %stack.2), calls=%async_computation | async-start | bytes 2097152 | tf_op jit(solution)/shard_map/all_to_all | solution.py:29
  16.8 2.5 %collective-permute-start = (s32[8]{0:T(128)S(1)}, s32[8]{0:T(128)S(1)}, u32[]{:S(2)}, u32[]{:S(2)}) collective-permute-start(s32[8]{0:T(128)S(1)} %get-tuple-element.35), channel_id=1, source_target_pairs={{8,0},{12,4},{16,8},{20,12},{24,16},{28,20},{0,24},{4,28},{9,1},{1... | collective-permute-start | bytes 104 | tf_op jit(solution)/shard_map/ppermute | solution.py:10
  26.2 16.3 %all-to-all-done = bf16[4,1024,128]{1,2,0:T(8,128)(2,1)S(1)} async-done(((bf16[4,1024,128]{1,2,0:T(8,128)(2,1)}), bf16[4,1024,128]{1,2,0:T(8,128)(2,1)S(1)}, u32[]{:S(2)}, u32[]{:S(2)}) %all-to-all-start) | async-done | bytes 1048608 | tf_op jit(solution)/shard_map/all_to_all | solution.py:29
  44.4 1.5 collective-permute-start.1
  49.8 1.4 broadcast_select_fusion.2
  51.9 1.4 broadcast_select_fusion.1
  53.3 2.6 %collective-permute-start.5 = (bf16[8,128,128]{2,1,0:T(8,128)(2,1)}, bf16[8,128,128]{2,1,0:T(8,128)(2,1)}, u32[]{:S(2)}, u32[]{:S(2)}) collective-permute-start(bf16[8,128,128]{2,1,0:T(8,128)(2,1)} %broadcast_select_fusion.1), channel_id=1, source_target_pairs={{4,0},{8,4},{12,8},{16,12},{20,16},{24,20},{28,24},{0,28},{5,1},{9... | collective-permute-start | bytes 786440 | tf_op jit(solution)/shard_map/ppermute | solution.py:10
  56.6 1.4 broadcast_select_fusion
  61.0 2.1 %fusion.21 = f32[8,128,128]{2,1,0:T(8,128)} fusion(bf16[8,128,128]{2,1,0:T(8,128)(2,1)} %collective-permute-done.3, bf16[1,5,8,128,128]{4,3,2,1,0:T(8,128)(2,1)S(1)} %copy-done.1), kind=kOutput, calls=%fused_computation.48 | convolution fusion | flops 33554432 | bytes 1048576 | tf_op jit(solution)/shard_map/sij,sjf->sif/dot_general | solution.py:48
  64.1 2.1 %copy.19 = f32[8,128,128]{1,0,2:T(8,128)} copy(f32[8,128,128]{2,1,0:T(8,128)} %fusion.21) | data formatting | bytes 1048576 | tf_op jit(solution)/shard_map/sij,sjf->sif/dot_general | solution.py:48
  66.1 1.3 fusion.17
  69.5 2.0 %copy.21 = f32[8,128,128]{1,0,2:T(8,128)} copy(f32[8,128,128]{2,1,0:T(8,128)} %fusion.13) | data formatting | bytes 1048576 | tf_op jit(solution)/shard_map/sij,sjf->sif/dot_general | solution.py:48
  71.6 1.5 convolution_add_fusion.5
  78.3 1.9 %multiply_bitcast_fusion.3 = f32[8,128,128]{2,0,1:T(8,128)} fusion(f32[8,128,128]{1,0,2:T(8,128)} %copy.23, f32[8]{0:T(128)S(1)} %copy-done.13), kind=kLoop, calls=%fused_computation.34 | loop fusion | flops 131072 | bytes 1048608 | tf_op jit(solution)/shard_map/mul | solution.py:76
  80.2 2.5 %collective-permute-start.8 = (f32[8,128,128]{2,0,1:T(8,128)}, f32[8,128,128]{2,0,1:T(8,128)}, u32[]{:S(2)}, u32[]{:S(2)}) collective-permute-start(f32[8,128,128]{2,0,1:T(8,128)} %multiply_bitcast_fusion.3), channel_id=1, source_target_pairs={{8,0},{12,4},{16,8},{20,12},{24,16},{28,20},{0,24},{4,28},{9,1},{1... | collective-permute-start | bytes 1572872 | tf_op jit(solution)/shard_map/ppermute | solution.py:10
  83.3 1.4 gather_fusion.8
  84.7 1.3 fusion.15
  87.0 1.9 %multiply_bitcast_fusion.1 = f32[8,128,128]{2,0,1:T(8,128)} fusion(f32[8,128,128]{1,0,2:T(8,128)} %copy.25, f32[8]{0:T(128)S(1)} %copy-done.12), kind=kLoop, calls=%fused_computation.32 | loop fusion | flops 131072 | bytes 1048608 | tf_op jit(solution)/shard_map/mul | solution.py:76
  89.0 1.5 gather_fusion.9
  90.5 1.3 fusion.11
  92.8 1.9 %multiply_bitcast_fusion = f32[8,128,128]{2,0,1:T(8,128)} fusion(f32[8,128,128]{1,0,2:T(8,128)} %copy.26, f32[8]{0:T(128)S(1)} %copy-done.11), kind=kLoop, calls=%fused_computation.31 | loop fusion | flops 131072 | bytes 1048608 | tf_op jit(solution)/shard_map/mul | solution.py:76
  94.8 1.4 gather_fusion.7
  96.6 2.1 %fusion.19 = f32[8,128,128]{2,1,0:T(8,128)} fusion(bf16[8,128,128]{2,1,0:T(8,128)(2,1)} %gather_fusion.7, pred[8]{0:T(512)(128)(4,1)S(1)} %copy-done.14, bf16[1,5,8,128,128]{4,3,2,1,0:T(8,128)(2,1)S(1)} %copy-done.1), kind=kOutput, calls=%fused_computation.46 | convolution fusion | flops 33685504 | bytes 1049088 | tf_op jit(solution)/shard_map/sji,sjf->sif/dot_general | solution.py:63
  100.3 2.9 %collective-permute-start.9 = (f32[8,128,128]{2,0,1:T(8,128)S(1)}, f32[8,128,128]{2,0,1:T(8,128)S(1)}, u32[]{:S(2)}, u32[]{:S(2)}) collective-permute-start(f32[8,128,128]{2,0,1:T(8,128)S(1)} %multiply_bitcast_fusion.2), channel_id=1, source_target_pairs={{4,0},{8,4},{12,8},{16,12},{20,16},{24,20},{28,24},{0,28},{5,1},{9... | collective-permute-start | bytes 1572872 | tf_op jit(solution)/shard_map/ppermute | solution.py:10
  103.6 1.4 fusion.65
  105.0 5.8 %collective-permute-done.11 = f32[8,128,128]{2,0,1:T(8,128)} collective-permute-done((f32[8,128,128]{2,0,1:T(8,128)}, f32[8,128,128]{2,0,1:T(8,128)}, u32[]{:S(2)}, u32[]{:S(2)}) %collective-permute-start.11) | collective-permute-done | bytes 524320 | tf_op jit(solution)/shard_map/ppermute | solution.py:10
  110.8 1.4 fusion.68
  112.2 1.4 convolution_add_fusion.1
  116.2 1.8 fusion.89
  118.0 51.8 %all-reduce.2.cloned.1.call-done = f32[512,128]{0,1:T(8,128)} async-done(((f32[512,128]{0,1:T(8,128)}), f32[512,128]{0,1:T(8,128)}) %all-reduce.2.cloned.1.call-update) | async-done | bytes 262160 | tf_op jit(solution)/shard_map/psum | solution.py:90
  169.8 1.8 copy.16
  171.6 1.8 convert_element_type.89
  (142 shorter events, 35.0 us)
Async XLA Ops:
  8.0 34.5 %copy-start = (bf16[512,128]{1,0:T(8,128)(2,1)S(1)}, bf16[512,128]{1,0:T(8,128)(2,1)}, u32[]{:S(2)}) copy-start(bf16[512,128]{1,0:T(8,128)(2,1)} %param.10) | copy-start | bytes 393220
  10.3 6.5 %copy-start.8 = (s32[1,5,8]{2,0,1:T(1,128)S(1)}, s32[1,5,8]{2,0,1:T(1,128)}, u32[]{:S(2)}) copy-start(s32[1,5,8]{2,0,1:T(1,128)} %param.13) | copy-start | bytes 484
  10.3 9.9 %copy-start.7 = (s32[1,5,8]{2,0,1:T(1,128)S(1)}, s32[1,5,8]{2,0,1:T(1,128)}, u32[]{:S(2)}) copy-start(s32[1,5,8]{2,0,1:T(1,128)} %param.12) | copy-start | bytes 484
  10.3 10.5 %copy-start.28 = (s32[1,5]{1,0:T(1,128)S(1)}, s32[1,5]{1,0:T(1,128)}, u32[]{:S(2)}) copy-start(s32[1,5]{1,0:T(1,128)} %param.14) | copy-start | bytes 64
  10.3 32.2 %all-to-all-start = ((bf16[4,1024,128]{1,2,0:T(8,128)(2,1)}), bf16[4,1024,128]{1,2,0:T(8,128)(2,1)S(1)}, u32[]{:S(2)}, u32[]{:S(2)}) async-start(bf16[4,1024,128]{1,2,0:T(8,128)(2,1)} %stack.2), calls=%async_computation | async-start | bytes 2097152 | tf_op jit(solution)/shard_map/all_to_all | solution.py:29
  16.7 153.1 %all-reduce.2.cloned.1.call-start = ((), (), s32[]{:S(2)}) async-start(), calls=%async_computation.3 | async-start | bytes 524288 | tf_op jit(solution)/shard_map/psum | solution.py:90
  16.8 6.6 %collective-permute-start = (s32[8]{0:T(128)S(1)}, s32[8]{0:T(128)S(1)}, u32[]{:S(2)}, u32[]{:S(2)}) collective-permute-start(s32[8]{0:T(128)S(1)} %get-tuple-element.35), channel_id=1, source_target_pairs={{8,0},{12,4},{16,8},{20,12},{24,16},{28,20},{0,24},{4,28},{9,1},{1... | collective-permute-start | bytes 104 | tf_op jit(solution)/shard_map/ppermute | solution.py:10
  19.3 4.1 %collective-permute-start.2 = (s32[8]{0:T(128)S(1)}, s32[8]{0:T(128)S(1)}, u32[]{:S(2)}, u32[]{:S(2)}) collective-permute-start(s32[8]{0:T(128)S(1)} %get-tuple-element.34), channel_id=1, source_target_pairs={{4,0},{8,4},{12,8},{16,12},{20,16},{24,20},{28,24},{0,28},{5,1},{9... | collective-permute-start | bytes 104 | tf_op jit(solution)/shard_map/ppermute | solution.py:10
  19.3 4.7 %collective-permute-start.4 = (s32[8]{0:T(128)S(1)}, s32[8]{0:T(128)S(1)}, u32[]{:S(2)}, u32[]{:S(2)}) collective-permute-start(s32[8]{0:T(128)S(1)} %get-tuple-element.33), channel_id=1, source_target_pairs={{28,0},{0,4},{4,8},{8,12},{12,16},{16,20},{20,24},{24,28},{29,1},{... | collective-permute-start | bytes 104 | tf_op jit(solution)/shard_map/ppermute | solution.py:10
  19.8 4.8 %collective-permute-start.6 = (s32[8]{0:T(128)S(1)}, s32[8]{0:T(128)S(1)}, u32[]{:S(2)}, u32[]{:S(2)}) collective-permute-start(s32[8]{0:T(128)S(1)} %get-tuple-element.32), channel_id=1, source_target_pairs={{24,0},{28,4},{0,8},{4,12},{8,16},{12,20},{16,24},{20,28},{25,1},{... | collective-permute-start | bytes 104 | tf_op jit(solution)/shard_map/ppermute | solution.py:10
  23.3 23.2 %copy-start.20 = (s32[8]{0:T(128)}, s32[8]{0:T(128)S(1)}, u32[]{:S(2)}) copy-start(s32[8]{0:T(128)S(1)} %collective-permute-done) | copy-start | bytes 100
  23.3 23.1 %copy-start.26 = (s32[8]{0:T(128)}, s32[8]{0:T(128)S(1)}, u32[]{:S(2)}) copy-start(s32[8]{0:T(128)S(1)} %collective-permute-done.2) | copy-start | bytes 100
  24.0 22.5 %copy-start.24 = (s32[8]{0:T(128)}, s32[8]{0:T(128)S(1)}, u32[]{:S(2)}) copy-start(s32[8]{0:T(128)S(1)} %collective-permute-done.4) | copy-start | bytes 100
  24.6 21.9 %copy-start.22 = (s32[8]{0:T(128)}, s32[8]{0:T(128)S(1)}, u32[]{:S(2)}) copy-start(s32[8]{0:T(128)S(1)} %collective-permute-done.6) | copy-start | bytes 100
  42.5 4.0 %copy-start.1 = (bf16[1,5,8,128,128]{4,3,2,1,0:T(8,128)(2,1)S(1)}, bf16[1,5,8,128,128]{4,3,2,1,0:T(8,128)(2,1)}, u32[]{:S(2)}) copy-start(bf16[1,5,8,128,128]{4,3,2,1,0:T(8,128)(2,1)} %param.11) | copy-start | bytes 3932164
  44.4 15.3 %collective-permute-start.1 = (bf16[8,128,128]{2,1,0:T(8,128)(2,1)}, bf16[8,128,128]{2,1,0:T(8,128)(2,1)}, u32[]{:S(2)}, u32[]{:S(2)}) collective-permute-start(bf16[8,128,128]{2,1,0:T(8,128)(2,1)} %broadcast_select_fusion.3), channel_id=1, source_target_pairs={{24,0},{28,4},{0,8},{4,12},{8,16},{12,20},{16,24},{20,28},{25,1},{... | collective-permute-start | bytes 786440 | tf_op jit(solution)/shard_map/ppermute | solution.py:10
  51.2 9.8 %collective-permute-start.3 = (bf16[8,128,128]{2,1,0:T(8,128)(2,1)}, bf16[8,128,128]{2,1,0:T(8,128)(2,1)}, u32[]{:S(2)}, u32[]{:S(2)}) collective-permute-start(bf16[8,128,128]{2,1,0:T(8,128)(2,1)} %broadcast_select_fusion.2), channel_id=1, source_target_pairs={{28,0},{0,4},{4,8},{8,12},{12,16},{16,20},{20,24},{24,28},{29,1},{... | collective-permute-start | bytes 786440 | tf_op jit(solution)/shard_map/ppermute | solution.py:10
  53.3 12.8 %collective-permute-start.5 = (bf16[8,128,128]{2,1,0:T(8,128)(2,1)}, bf16[8,128,128]{2,1,0:T(8,128)(2,1)}, u32[]{:S(2)}, u32[]{:S(2)}) collective-permute-start(bf16[8,128,128]{2,1,0:T(8,128)(2,1)} %broadcast_select_fusion.1), channel_id=1, source_target_pairs={{4,0},{8,4},{12,8},{16,12},{20,16},{24,20},{28,24},{0,28},{5,1},{9... | collective-permute-start | bytes 786440 | tf_op jit(solution)/shard_map/ppermute | solution.py:10
  58.0 10.4 %collective-permute-start.7 = (bf16[8,128,128]{2,1,0:T(8,128)(2,1)}, bf16[8,128,128]{2,1,0:T(8,128)(2,1)S(1)}, u32[]{:S(2)}, u32[]{:S(2)}) collective-permute-start(bf16[8,128,128]{2,1,0:T(8,128)(2,1)} %broadcast_select_fusion), channel_id=1, source_target_pairs={{8,0},{12,4},{16,8},{20,12},{24,16},{28,20},{0,24},{4,28},{9,1},{1... | collective-permute-start | bytes 786440 | tf_op jit(solution)/shard_map/ppermute | solution.py:10
  78.3 6.4 %copy-start.17 = (pred[8]{0:T(512)(128)(4,1)S(1)}, pred[8]{0:T(512)(128)(4,1)}, u32[]{:S(2)}) copy-start(pred[8]{0:T(512)(128)(4,1)} %get-tuple-element.30) | copy-start | bytes 28
  80.2 32.0 %collective-permute-start.8 = (f32[8,128,128]{2,0,1:T(8,128)}, f32[8,128,128]{2,0,1:T(8,128)}, u32[]{:S(2)}, u32[]{:S(2)}) collective-permute-start(f32[8,128,128]{2,0,1:T(8,128)} %multiply_bitcast_fusion.3), channel_id=1, source_target_pairs={{8,0},{12,4},{16,8},{20,12},{24,16},{28,20},{0,24},{4,28},{9,1},{1... | collective-permute-start | bytes 1572872 | tf_op jit(solution)/shard_map/ppermute | solution.py:10
  83.3 3.7 %copy-start.12 = (f32[8]{0:T(128)S(1)}, f32[8]{0:T(128)}, u32[]{:S(2)}) copy-start(f32[8]{0:T(128)} %get-tuple-element.39) | copy-start | bytes 100
  86.0 4.5 %copy-start.16 = (pred[8]{0:T(512)(128)(4,1)S(1)}, pred[8]{0:T(512)(128)(4,1)}, u32[]{:S(2)}) copy-start(pred[8]{0:T(512)(128)(4,1)} %get-tuple-element.28) | copy-start | bytes 28
  89.0 14.6 %collective-permute-start.10 = (f32[8,128,128]{2,0,1:T(8,128)}, f32[8,128,128]{2,0,1:T(8,128)}, u32[]{:S(2)}, u32[]{:S(2)}) collective-permute-start(f32[8,128,128]{2,0,1:T(8,128)} %multiply_bitcast_fusion.1), channel_id=1, source_target_pairs={{28,0},{0,4},{4,8},{8,12},{12,16},{16,20},{20,24},{24,28},{29,1},{... | collective-permute-start | bytes 1572872 | tf_op jit(solution)/shard_map/ppermute | solution.py:10
  89.0 3.9 %copy-start.11 = (f32[8]{0:T(128)S(1)}, f32[8]{0:T(128)}, u32[]{:S(2)}) copy-start(f32[8]{0:T(128)} %get-tuple-element.38) | copy-start | bytes 100
  91.8 4.4 %copy-start.15 = (pred[8]{0:T(512)(128)(4,1)S(1)}, pred[8]{0:T(512)(128)(4,1)}, u32[]{:S(2)}) copy-start(pred[8]{0:T(512)(128)(4,1)} %get-tuple-element.26) | copy-start | bytes 28
  94.8 16.0 %collective-permute-start.11 = (f32[8,128,128]{2,0,1:T(8,128)}, f32[8,128,128]{2,0,1:T(8,128)}, u32[]{:S(2)}, u32[]{:S(2)}) collective-permute-start(f32[8,128,128]{2,0,1:T(8,128)} %multiply_bitcast_fusion), channel_id=1, source_target_pairs={{24,0},{28,4},{0,8},{4,12},{8,16},{12,20},{16,24},{20,28},{25,1},{... | collective-permute-start | bytes 1572872 | tf_op jit(solution)/shard_map/ppermute | solution.py:10
  100.3 10.5 %copy-start.23 = (s32[8]{0:T(128)S(1)}, s32[8]{0:T(128)}, u32[]{:S(2)}) copy-start(s32[8]{0:T(128)} %copy-done.22) | copy-start | bytes 100
  100.3 14.0 %collective-permute-start.9 = (f32[8,128,128]{2,0,1:T(8,128)S(1)}, f32[8,128,128]{2,0,1:T(8,128)S(1)}, u32[]{:S(2)}, u32[]{:S(2)}) collective-permute-start(f32[8,128,128]{2,0,1:T(8,128)S(1)} %multiply_bitcast_fusion.2), channel_id=1, source_target_pairs={{4,0},{8,4},{12,8},{16,12},{20,16},{24,20},{28,24},{0,28},{5,1},{9... | collective-permute-start | bytes 1572872 | tf_op jit(solution)/shard_map/ppermute | solution.py:10
  103.6 8.6 %copy-start.21 = (s32[8]{0:T(128)S(1)}, s32[8]{0:T(128)}, u32[]{:S(2)}) copy-start(s32[8]{0:T(128)} %copy-done.20) | copy-start | bytes 100
  105.0 9.4 %copy-start.27 = (s32[8]{0:T(128)S(1)}, s32[8]{0:T(128)}, u32[]{:S(2)}) copy-start(s32[8]{0:T(128)} %copy-done.26) | copy-start | bytes 100
  116.2 55.4 %reduce-scatter.2.cloned.1.call-start = ((), (), s32[]{:S(2)}) async-start(), calls=%async_computation.2 | async-start | bytes 2621440 | tf_op jit(solution)/shard_map/reduce_scatter | solution.py:94
  (12 other events, 29.8 us)
Sparse Core Ops, SparseCore 0:
  116.3 53.4 all-reduce.1
Sparse Core Ops, SparseCore 1:
  119.0 43.1 reduce-scatter.1
